TPU v7x, 32 devices: a whole 2x2x4 slice. The times are simulated.
32 devices in a mesh: grp: 2 (over x), node: 16 (over z, y, core).
Axes of the slice: x: 2, y: 2, z: 4, core: 2. Of those that a mesh axis runs over, the one named last changes fastest.
Arguments:
- nodes: bfloat16 [128, 2, 1024, 1024], P('grp', None, 'node'), parts along dimension 0, may hold values from -0.34960938 to 0.34960938
- pair_nodes: int32 [16, 2], replicated, may hold values from 0 to 63
- prod_left: int32 [16], replicated, may hold values from 0 to 15, as said below
- prod_right: int32 [16], replicated, may hold values from 0 to 15, each once
- prod_flag: int32 [16], replicated, may hold values from 0 to 1
- prod_diag: int32 [16], replicated, may hold values from 0 to 7, as said below
Outputs:
- diagrams: bfloat16 [16, 2, 1024, 1024], P('grp', None, 'node'), parts along dimension 0
There are 2 independent parts, one for each index of `grp`. A program takes and returns all parts, laid end to end along the dimension named above; an argument that names none is the same for every part. Nothing has to cross between parts.
Inputs may be any that keep to these rules, and one draw needn't show every extreme that they name: `prod_left`: exactly 8 distinct pairs are left operands, each of exactly two products. `prod_diag`: every diagram receives exactly two products.
All inputs are finite; a program needn't handle non-finite values.
Results may differ from a plain program's by a relative error of at most 0.0065.
Values may be sent and summed in bfloat16 or wider, within the bound.
A program may use at most 128 MiB of HBM per device.

v0:
```python
import functools

import jax
import jax.numpy as jnp
from jax import lax
from jax.experimental import pallas as pl
from jax.experimental.pallas import tpu as pltpu
from jax.sharding import PartitionSpec as P

TILE = 256
AHEAD = 4
WIDTH = 128


def plan_and_gather_kernel(
    graph,
    nodes,
    flags,
    merges,
    finals,
    left_out,
    a_out,
    b_out,
    seen_left,
    seen_diag,
    mate_left,
    mate_diag,
    done,
    slot_of,
    order,
    left_sem,
    a_sem,
    b_sem,
):
    count = graph.shape[1]
    diags = count // 2
    half = count // 2
    first_node, prod_left, prod_right, prod_flag, prod_diag = 0, 2, 3, 4, 5
    slots = half // 2 + 1
    chunks = b_out.shape[0]
    width = b_out.shape[-1]

    @pl.loop(0, count)
    def _(p):
        seen_left[p] = -1

    @pl.loop(0, diags)
    def _(d):
        seen_diag[d] = -1
        slot_of[d] = -1
        slot_of[diags + d] = -1

    @pl.loop(0, count)
    def _(k):
        done[k] = 0
        for group, seen, mate in (
            (graph[prod_left, k], seen_left, mate_left),
            (graph[prod_diag, k], seen_diag, mate_diag),
        ):
            earlier = seen[group]
            found = earlier >= 0
            mate[k] = earlier
            back = jnp.where(found, earlier, k)
            mate[back] = jnp.where(found, k, mate[back])
            seen[group] = k

    def place(g, now):
        other = mate_left[now]
        done[now] = 1
        done[other] = 1
        order[2 * g] = now
        order[2 * g + 1] = other
        for side, k in ((first_node, now), (first_node + 1, other)):
            at = 2 * g + side
            flags[at] = graph[prod_flag, k]
            left_id = graph[side, graph[prod_left, k]]
            right = graph[prod_right, k]
            pltpu.make_async_copy(nodes.at[left_id], left_out.at[at], left_sem).start()
            pltpu.make_async_copy(nodes.at[graph[first_node, right]], a_out.at[at], a_sem).start()
            for c in range(chunks):
                pltpu.make_async_copy(
                    nodes.at[graph[first_node + 1, right], :, :, pl.ds(c * width, width)],
                    b_out.at[c, at],
                    b_sem,
                ).start()
        free = lax.fori_loop(
            0,
            count,
            lambda k, best: jnp.where(done[count - 1 - k] == 0, count - 1 - k, best),
            jnp.int32(0),
            unroll=True,
        )
        follow = mate_diag[other]
        return jnp.where(done[follow] == 0, follow, free)

    lax.fori_loop(0, count // 2, place, jnp.int32(0))

    for h in range(2):
        base = h * slots

        @pl.loop(0, slots)
        def _(t):
            merges[2 * (base + t)] = half
            merges[2 * (base + t) + 1] = half

        def take(i, used):
            diag = graph[prod_diag, order[h * half + i]]
            slot = slot_of[h * diags + diag]
            new = slot < 0
            slot = jnp.where(new, used, slot)
            slot_of[h * diags + diag] = slot
            at = 2 * (base + slot)
            merges[at] = jnp.where(new, i, merges[at])
            merges[at + 1] = jnp.where(new, half, i)
            return used + new.astype(jnp.int32)

        lax.fori_loop(0, half, take, jnp.int32(0))

    for h in range(2):

        @pl.loop(0, diags)
        def _(d):
            near = slot_of[h * diags + d]
            far = half + slot_of[(1 - h) * diags + d]
            here = near >= 0
            at = 2 * (h * slots + jnp.maximum(near, 0))
            both = here & (merges[at + 1] < half)
            finals[2 * (h * diags + d)] = jnp.where(here, merges[at], far)
            finals[2 * (h * diags + d) + 1] = jnp.where(
                both, merges[at + 1], jnp.where(here, far, half + slots)
            )

    pltpu.make_async_copy(left_out, left_out, left_sem).wait()
    pltpu.make_async_copy(a_out, a_out, a_sem).wait()
    pltpu.make_async_copy(b_out, b_out, b_sem).wait()


def plan_and_gather(nodes, pair_nodes, prod_left, prod_right, prod_flag, prod_diag, chunks):
    count = prod_left.shape[0]
    _, parts, rows, order = nodes.shape
    half = count // 2
    slots = half // 2 + 1
    whole = jax.ShapeDtypeStruct((count, parts, rows, order), nodes.dtype)
    graph = jnp.stack(
        [pair_nodes[:, 0], pair_nodes[:, 1], prod_left, prod_right, prod_flag, prod_diag]
    )
    cut = jax.ShapeDtypeStruct((chunks, count, parts, rows, order // chunks), nodes.dtype)
    table = lambda size: jax.ShapeDtypeStruct((size,), jnp.int32)
    smem = pl.BlockSpec(memory_space=pltpu.SMEM)
    scratch = lambda size: pltpu.SMEM((size,), jnp.int32)
    return pl.pallas_call(
        plan_and_gather_kernel,
        out_shape=(table(count), table(4 * slots), table(4 * half), whole, whole, cut),
        in_specs=[smem, pl.BlockSpec(memory_space=pltpu.HBM)],
        out_specs=[smem] * 3 + [pl.BlockSpec(memory_space=pltpu.VMEM)] * 3,
        scratch_shapes=[
            scratch(count),
            scratch(half),
            scratch(count),
            scratch(count),
            scratch(count),
            scratch(2 * half),
            scratch(count),
            pltpu.SemaphoreType.DMA,
            pltpu.SemaphoreType.DMA,
            pltpu.SemaphoreType.DMA,
        ],
        compiler_params=pltpu.CompilerParams(vmem_limit_bytes=36 * 2**20),
    )(graph, nodes)


def tile_product(left_re, left_im, right_re, right_im):
    dot = functools.partial(jnp.dot, preferred_element_type=jnp.float32)
    real_part = dot(left_re, right_re) - dot(left_im, right_im)
    imag_part = dot(left_re, right_im) + dot(left_im, right_re)
    return real_part.astype(jnp.bfloat16), imag_part.astype(jnp.bfloat16)


def exchange_kernel(
    n,
    flags,
    merges,
    finals,
    left_send,
    a_send,
    b_send,
    out,
    lefts,
    a_full,
    b_full,
    left_plain,
    left_used,
    right_pair,
    result,
    panels,
    relayed,
    merged,
    left_sem,
    a_sem,
    b_sem,
    swap_sem,
    result_sem,
    relay_sem,
    far_sem,
    left_out_sem,
    a_out_sem,
    b_out_sem,
    swap_out_sem,
    result_out_sem,
    relay_out_sem,
    far_out_sem,
):
    me = lax.axis_index("node")
    parity = lax.rem(me, 2)
    partner = me + 1 - 2 * parity
    chunks = b_full.shape[0]
    order = a_full.shape[1]
    rows = left_send.shape[2]
    tiles = order // TILE
    my_rows = pl.ds(pl.multiple_of(me * rows, rows), rows)

    def target(t):
        half = lax.div(t + 1, 2)
        return lax.rem(me + n // 2 + (2 * lax.rem(t, 2) - 1) * half, n)

    barrier = pltpu.get_barrier_semaphore()

    @pl.loop(0, n - 1)
    def _(t):
        pl.semaphore_signal(
            barrier,
            inc=1,
            device_id={"node": target(t)},
            device_id_type=pl.DeviceIdType.MESH,
        )

    pl.semaphore_wait(barrier, n - 1)

    def push(src, dst, send_sem, recv_sem, to):
        pltpu.make_async_remote_copy(
            src_ref=src,
            dst_ref=dst,
            send_sem=send_sem,
            recv_sem=recv_sem,
            device_id={"node": to},
            device_id_type=pl.DeviceIdType.MESH,
        ).start()

    def landed(ref, sem):
        pltpu.make_async_copy(ref, ref, sem).wait()

    @pl.loop(0, n - 1)
    def _(t):
        to = target(t)
        push(left_send.at[to], lefts.at[lax.rem(to, 2), :, my_rows], left_out_sem, left_sem, to)

    pltpu.make_async_copy(left_send.at[me], lefts.at[parity, :, my_rows], left_sem).start()

    @pl.loop(0, n - 1)
    def _(t):
        to = target(t)
        push(a_send.at[to], a_full.at[:, my_rows], a_out_sem, a_sem, to)

    pltpu.make_async_copy(a_send.at[me], a_full.at[:, my_rows], a_sem).start()

    def push_right(c):
        @pl.loop(0, n - 1)
        def _(t):
            to = target(t)
            push(b_send.at[c, to], b_full.at[c, :, my_rows], b_out_sem.at[c], b_sem.at[c], to)

        pltpu.make_async_copy(b_send.at[c, me], b_full.at[c, :, my_rows], b_sem.at[c]).start()

    for c in range(min(AHEAD, chunks)):
        push_right(c)

    landed(lefts.at[parity], left_sem)
    push(lefts.at[parity], lefts.at[parity], swap_out_sem, swap_sem, partner)
    landed(lefts.at[1 - parity], swap_sem)

    def block(i):
        return pl.ds(pl.multiple_of(i * TILE, TILE), TILE)

    @pl.loop(0, tiles * tiles)
    def _(t):
        down, across = block(lax.div(t, tiles)), block(lax.rem(t, tiles))
        real_part, imag_part = tile_product(
            lefts[0, 0, down, :], lefts[0, 1, down, :], lefts[1, 0, :, across], lefts[1, 1, :, across]
        )
        left_plain[0, down, across] = real_part
        left_plain[1, down, across] = imag_part

    half = n // 2
    slots = merged.shape[1]
    near, far = pl.ds(0, half), pl.ds(half, slots)
    side, place = lax.div(me, half), lax.rem(me, half)
    mirror = lax.rem(me + half, n)

    def rows_of(device):
        return pl.ds(pl.multiple_of(device * rows, rows), rows)

    for c in range(chunks):
        panels[c][half + slots] = jnp.zeros(panels[c].shape[1:], panels[c].dtype)
        relayed[c][half] = jnp.zeros(relayed[c].shape[1:], relayed[c].dtype)

    flipped = flags[me] == 1

    @pl.loop(0, tiles * tiles)
    def _(t):
        down, across = block(lax.div(t, tiles)), block(lax.rem(t, tiles))
        left_used[0, down, across] = jnp.where(
            flipped, left_plain[0, across, down].T, left_plain[0, down, across]
        )
        left_used[1, down, across] = jnp.where(
            flipped, -left_plain[1, across, down].T, left_plain[1, down, across]
        )

    landed(a_full, a_sem)

    def compute(c):
        landed(b_full.at[c], b_sem.at[c])

        @pl.loop(0, tiles)
        def _(i):
            down = block(i)
            real_part, imag_part = tile_product(
                a_full[0, down, :], a_full[1, down, :], b_full[c, 0], b_full[c, 1]
            )
            right_pair[0, down, :] = real_part
            right_pair[1, down, :] = imag_part

        @pl.loop(0, tiles)
        def _(i):
            down = block(i)
            real_part, imag_part = tile_product(
                left_used[0, down, :], left_used[1, down, :], right_pair[0], right_pair[1]
            )
            result[c, 0, down, :] = real_part
            result[c, 1, down, :] = imag_part

        @pl.loop(1, half)
        def _(t):
            to = side * half + lax.rem(place + t, half)
            push(
                result.at[c, :, rows_of(lax.rem(to + half, n))],
                relayed[c].at[place],
                relay_out_sem.at[c],
                relay_sem.at[c],
                to,
            )

        pltpu.make_async_copy(
            result.at[c, :, rows_of(mirror)], relayed[c].at[place], relay_sem.at[c]
        ).start()

        @pl.loop(1, half)
        def _(t):
            to = side * half + lax.rem(place + t, half)
            push(
                result.at[c, :, rows_of(to)],
                panels[c].at[place],
                result_out_sem.at[c],
                result_sem.at[c],
                to,
            )

        pltpu.make_async_copy(
            result.at[c, :, my_rows], panels[c].at[place], result_sem.at[c]
        ).start()

    def merge(c):
        landed(relayed[c].at[near], relay_sem.at[c])

        @pl.loop(0, slots)
        def _(t):
            at = 2 * (side * slots + t)
            first = relayed[c][merges[at]].astype(jnp.float32)
            second = relayed[c][merges[at + 1]].astype(jnp.float32)
            merged[c, t] = (first + second).astype(merged.dtype)

        push(merged.at[c], panels[c].at[far], far_out_sem.at[c], far_sem.at[c], mirror)

    for c in range(chunks):
        compute(c)
        if c + AHEAD < chunks:
            push_right(c + AHEAD)
        if c > 0:
            merge(c - 1)
    merge(chunks - 1)

    width = b_full.shape[-1]
    for c in range(chunks):
        landed(panels[c].at[near], result_sem.at[c])
        landed(panels[c].at[far], far_sem.at[c])

        @pl.loop(0, out.shape[0])
        def _(d):
            at = 2 * (side * out.shape[0] + d)
            first = panels[c][finals[at]].astype(jnp.float32)
            second = panels[c][finals[at + 1]].astype(jnp.float32)
            out[d, :, :, c * width : (c + 1) * width] = (first + second).astype(out.dtype)

    others = pl.ds(0, n - 1)
    others_near = pl.ds(0, half - 1)
    landed(left_send.at[others], left_out_sem)
    landed(a_send.at[others], a_out_sem)
    landed(lefts.at[parity], swap_out_sem)
    for c in range(chunks):
        landed(b_send.at[c, others], b_out_sem.at[c])
        landed(panels[c].at[others_near], result_out_sem.at[c])
        landed(relayed[c].at[others_near], relay_out_sem.at[c])
        landed(merged.at[c], far_out_sem.at[c])


def local(nodes, pair_nodes, prod_left, prod_right, prod_flag, prod_diag, *, n):
    _, parts, rows, order = nodes.shape
    count = prod_left.shape[0]
    assert count == n == pair_nodes.shape[0] and rows * n == order
    half = diags = count // 2
    slots = half // 2 + 1
    chunks = order // WIDTH
    flags, merges, finals, left_send, a_send, b_send = plan_and_gather(
        nodes, pair_nodes, prod_left, prod_right, prod_flag, prod_diag, chunks
    )
    width = order // chunks
    kind = nodes.dtype
    dma = pltpu.SemaphoreType.DMA
    smem = pl.BlockSpec(memory_space=pltpu.SMEM)
    anywhere = pl.BlockSpec(memory_space=pl.ANY)
    return pl.pallas_call(
        functools.partial(exchange_kernel, n),
        out_shape=jax.ShapeDtypeStruct((diags, parts, rows, order), kind),
        in_specs=[smem, smem, smem, anywhere, anywhere, anywhere],
        out_specs=pl.BlockSpec(memory_space=pltpu.VMEM),
        scratch_shapes=[
            pltpu.VMEM((2, parts, order, order), kind),
            pltpu.VMEM((parts, order, order), kind),
            pltpu.VMEM((chunks, parts, order, width), kind),
            pltpu.VMEM((parts, order, order), kind),
            pltpu.VMEM((parts, order, order), kind),
            pltpu.VMEM((parts, order, width), kind),
            pltpu.VMEM((chunks, parts, order, width), kind),
            [pltpu.VMEM((half + slots + 1, parts, rows, width), kind)] * chunks,
            [pltpu.VMEM((half + 1, parts, rows, width), kind)] * chunks,
            pltpu.VMEM((chunks, slots, parts, rows, width), kind),
            dma,
            dma,
            dma((chunks,)),
            dma,
            dma((chunks,)),
            dma((chunks,)),
            dma((chunks,)),
            dma,
            dma,
            dma((chunks,)),
            dma,
            dma((chunks,)),
            dma((chunks,)),
            dma((chunks,)),
        ],
        compiler_params=pltpu.CompilerParams(
            collective_id=0, has_side_effects=True, vmem_limit_bytes=38 * 2**20
        ),
    )(flags, merges, finals, left_send, a_send, b_send)


def solution(mesh):
    placed = (P("grp", None, "node", None), P(), P(), P(), P(), P())
    return jax.shard_map(
        functools.partial(local, n=mesh.shape["node"]),
        mesh=mesh,
        in_specs=placed,
        out_specs=P("grp", None, "node", None),
        check_vma=False,
    )
```

profile of v0, /device:TPU:13, one launch (start us, length us, event | category | flops | bytes accessed | tf_op | source)
XLA Modules:
  0.0 345.8 jit_solution(11707573348124500910)
XLA Ops:
  0.0 0.8 slice_bitcast_fusion
  0.8 0.7 stack.19.graph
  1.5 6.6 %shard_map.64 = (s32[16]{0:T(128)S(1)}, s32[20]{0:T(128)S(1)}, s32[32]{0:T(128)S(1)}, bf16[16,2,64,1024]{3,2,1,0:T(8,128)(2,1)S(1)}, bf16[16,2,64,1024]{3,2,1,0:...) custom-call(s32[6,16]{1,0:T(8,128)S(1)} %stack.19.graph, bf16[64,2,64,1024]{3,2,1,0:T(8,128)(2,1)} %nodes.1), custom_call_target="tpu_custom_call" | custom-call | tf_op jit(solution)/shard_map/pallas_call | solution.py:151
  8.1 336.4 %shard_map.65 = bf16[8,2,64,1024]{3,2,1,0:T(8,128)(2,1)S(1)} custom-call(s32[16]{0:T(128)S(1)} %get-tuple-element.11.flags, s32[20]{0:T(128)S(1)} %get-tuple-element.12.merges, s32[32]{0:T(128)S(1)} %get-tuple-element.13.finals, bf16[16,2,64,1024]{3,2,1,0:T(8,128)(2,1)S(1)} %get-tuple-element.14.left_send, ...), custom_call_target="tpu_custom_call" | custom-call | tf_op jit(solution)/shard_map/pallas_call | solution.py:430
  344.5 1.3 copy.8
where the time goes:
time: 346 us
  Pallas kernels  343 us (99%)
    pallas_call x1, Pallas kernels, local(): pl.pallas_call(functools.partial(exchange_kernel, n), out_shape=jax.Shape...  336 us

commit v1 on v0

v1 whole, which is shorter than its diff:
```python
import functools

import jax
import jax.numpy as jnp
from jax import lax
from jax.experimental import pallas as pl
from jax.experimental.pallas import tpu as pltpu
from jax.sharding import PartitionSpec as P

TILE = 256
AHEAD = 8
WIDTH = 128
BAND = 16
LANES = 128


def searched(count):
    return 2 ** (count // 2 - 1) <= LANES


def plan_sizes(count):
    groups = count // 2
    if searched(count):
        return 3 * groups // 4, 3 * groups // 4
    return groups, groups


def choose_sides(graph, product, home, sides, group_of, extra, slots):
    groups = sides.shape[0]
    count = 2 * groups
    half = groups
    lane = lax.broadcasted_iota(jnp.int32, sides.shape, 1)
    group = lax.broadcasted_iota(jnp.int32, sides.shape, 0)
    sides[...] = lax.rem(lax.shift_right_logical(lane, group), 2).astype(jnp.float32)
    row = lambda g: sides[pl.ds(g, 1), :]
    zero = jnp.zeros((1, sides.shape[1]), jnp.float32)

    def add_group(g, carry):
        ones, inside_0, inside_1 = carry
        here = row(g)
        there = row(group_of[home[graph[2, product[2 * g]]]])
        return ones + here, inside_0 + (1 - here) * (1 - there), inside_1 + here * there

    ones, inside_0, inside_1 = lax.fori_loop(0, groups, add_group, (zero, zero, zero))

    def add_diag(k, carry):
        own_0, own_1 = carry
        k_mate = product[count + k]
        here, there = row(group_of[k]), row(group_of[k_mate])
        first = (k < k_mate).astype(jnp.float32)
        return own_0 + first * (1 - here * there), own_1 + first * jnp.maximum(here, there)

    own_0, own_1 = lax.fori_loop(0, count, add_diag, (zero, zero))
    new = half - jnp.minimum(inside_0, inside_1)
    own = jnp.maximum(own_0, own_1)
    bad = jnp.where(ones != groups // 2, 4096.0, 0.0)
    bad = bad + jnp.where(new > extra, 256.0, 0.0) + jnp.where(own > slots, 256.0, 0.0)
    cost = bad + 2 * new + own
    best = jnp.min(cost)
    index = lax.broadcasted_iota(jnp.int32, cost.shape, 1).astype(jnp.float32)
    return jnp.min(jnp.where(cost == best, index, 1e9)).astype(jnp.int32)


def plan_and_gather_kernel(
    n,
    graph,
    nodes,
    flags,
    left_slot,
    extra_slot,
    is_extra,
    merges,
    finals,
    left_own,
    a_own,
    b_own,
    left_cross,
    a_cross,
    b_cross,
    seen,
    group_of,
    product,
    home,
    chip_of,
    extras,
    used,
    slot_of,
    order,
    sides,
    early_sem,
    late_sem,
):
    count = graph.shape[1]
    groups = diags = half = count // 2
    extra = a_cross.shape[0]
    slots = merges.shape[0] // 4
    chunks = b_own.shape[0]
    width = b_own.shape[-1]
    first_node, prod_left, prod_right, prod_flag, prod_diag = 0, 2, 3, 4, 5
    me = lax.axis_index("node")
    side = lax.div(me, n // 2)

    @pl.loop(0, count)
    def _(p):
        seen[p] = -1
        seen[count + p] = -1
        chip_of[p] = -1

    @pl.loop(0, 2 * extra)
    def _(e):
        extras[e] = 0

    @pl.loop(0, 2 * diags)
    def _(d):
        slot_of[d] = -1

    def read(k, found):
        left = graph[prod_left, k]
        new = seen[left] < 0
        group = jnp.where(new, found, seen[left])
        seen[left] = group
        group_of[k] = group
        product[2 * group + 1] = k
        product[2 * group] = jnp.where(new, k, product[2 * group])
        home[graph[prod_right, k]] = k
        diag = graph[prod_diag, k]
        earlier = seen[count + diag]
        seen[count + diag] = k
        back = jnp.where(earlier < 0, k, earlier)
        product[count + k] = back
        product[count + back] = k
        return found + new.astype(jnp.int32)

    lax.fori_loop(0, count, read, jnp.int32(0))

    if not searched(count):
        mask = jnp.int32(2 ** (groups // 2) - 1)
    else:
        mask = choose_sides(graph, product, home, sides, group_of, extra, slots)

    def place(g, counts):
        which = lax.rem(lax.shift_right_logical(mask, g), 2)
        chip = jnp.where(which == 0, counts[0], groups // 2 + counts[1])
        order[2 * chip] = product[2 * g]
        order[2 * chip + 1] = product[2 * g + 1]
        chip_of[graph[prod_left, product[2 * g]]] = chip
        return counts[0] + 1 - which, counts[1] + which

    lax.fori_loop(0, groups, place, (jnp.int32(0), jnp.int32(0)))

    def read_node(node, dst, sem):
        pltpu.make_async_copy(nodes.at[node], dst, sem).start()

    def read_chunks(node, dst, at):
        for c in range(chunks):
            pltpu.make_async_copy(
                nodes.at[node, :, :, pl.ds(c * width, width)], dst.at[c, at], late_sem
            ).start()

    def left_node(k, at):
        return graph[lax.rem(at, 2), graph[prod_left, k]]

    @pl.loop(0, half)
    def _(i):
        read_node(left_node(order[(1 - side) * half + i], i), left_cross.at[i], early_sem)
        read_node(left_node(order[side * half + i], i), left_own.at[i], early_sem)

    used[0] = 0
    used[1] = 0

    @pl.loop(0, count)
    def _(at):
        which = lax.div(at, half)
        right = graph[prod_right, order[at]]
        chip = chip_of[right]
        local = (chip >= 0) & (lax.div(jnp.maximum(chip, 0), groups // 2) == which)
        spare = jnp.minimum(used[which], extra - 1)
        flags[at] = graph[prod_flag, order[at]]
        left_slot[at] = jnp.where(local, lax.rem(jnp.maximum(chip, 0), groups // 2), 0)
        extra_slot[at] = jnp.where(local, 0, spare)
        is_extra[at] = jnp.where(local, 0, 1)
        extras[which * extra + spare] = jnp.where(
            local, extras[which * extra + spare], right
        )
        used[which] = used[which] + jnp.where(local, 0, 1)

    @pl.loop(0, extra)
    def _(e):
        pair = extras[(1 - side) * extra + e]
        read_node(graph[first_node, pair], a_cross.at[e], early_sem)
        read_chunks(graph[first_node + 1, pair], b_cross, e)

    @pl.loop(0, half)
    def _(i):
        right = graph[prod_right, order[side * half + i]]
        read_node(graph[first_node, right], a_own.at[i], early_sem)
        read_chunks(graph[first_node + 1, right], b_own, i)

    for h in range(2):
        base = h * slots

        @pl.loop(0, slots)
        def _(t):
            merges[2 * (base + t)] = half
            merges[2 * (base + t) + 1] = half

        def take(i, taken):
            diag = graph[prod_diag, order[h * half + i]]
            slot = slot_of[h * diags + diag]
            new = slot < 0
            slot = jnp.where(new, jnp.minimum(taken, slots - 1), slot)
            slot_of[h * diags + diag] = slot
            at = 2 * (base + slot)
            merges[at] = jnp.where(new, i, merges[at])
            merges[at + 1] = jnp.where(new, half, i)
            return taken + new.astype(jnp.int32)

        lax.fori_loop(0, half, take, jnp.int32(0))

    for h in range(2):

        @pl.loop(0, diags)
        def _(d):
            near = slot_of[h * diags + d]
            far = half + slot_of[(1 - h) * diags + d]
            here = near >= 0
            at = 2 * (h * slots + jnp.maximum(near, 0))
            both = here & (merges[at + 1] < half)
            finals[2 * (h * diags + d)] = jnp.where(here, merges[at], far)
            finals[2 * (h * diags + d) + 1] = jnp.where(
                both, merges[at + 1], jnp.where(here, far, half + slots)
            )

    for ref in (left_own, a_own, left_cross, a_cross):
        pltpu.make_async_copy(ref, ref, early_sem).wait()
    for ref in (b_own, b_cross):
        pltpu.make_async_copy(ref, ref, late_sem).wait()


def plan_and_gather(n, nodes, pair_nodes, prod_left, prod_right, prod_flag, prod_diag, chunks):
    count = prod_left.shape[0]
    _, parts, rows, order = nodes.shape
    half = groups = count // 2
    extra, slots = plan_sizes(count)
    width = order // chunks
    graph = jnp.stack(
        [pair_nodes[:, 0], pair_nodes[:, 1], prod_left, prod_right, prod_flag, prod_diag]
    )
    whole = lambda size: jax.ShapeDtypeStruct((size, parts, rows, order), nodes.dtype)
    cut = lambda size: jax.ShapeDtypeStruct((chunks, size, parts, rows, width), nodes.dtype)
    table = lambda size: jax.ShapeDtypeStruct((size,), jnp.int32)
    smem = pl.BlockSpec(memory_space=pltpu.SMEM)
    scratch = lambda size: pltpu.SMEM((size,), jnp.int32)
    return pl.pallas_call(
        functools.partial(plan_and_gather_kernel, n),
        out_shape=(
            table(count),
            table(count),
            table(count),
            table(count),
            table(4 * slots),
            table(4 * half),
            whole(half),
            whole(half),
            cut(half),
            whole(half),
            whole(extra),
            cut(extra),
        ),
        in_specs=[smem, pl.BlockSpec(memory_space=pltpu.HBM)],
        out_specs=[smem] * 6 + [pl.BlockSpec(memory_space=pltpu.VMEM)] * 6,
        scratch_shapes=[
            scratch(2 * count),
            scratch(count),
            scratch(2 * count),
            scratch(count),
            scratch(count),
            scratch(2 * extra),
            scratch(2),
            scratch(2 * half),
            scratch(count),
            pltpu.VMEM((groups, LANES), jnp.float32),
            pltpu.SemaphoreType.DMA,
            pltpu.SemaphoreType.DMA,
        ],
        compiler_params=pltpu.CompilerParams(vmem_limit_bytes=36 * 2**20),
    )(graph, nodes)


def tile_product(left_re, left_im, right_re, right_im):
    dot = functools.partial(jnp.dot, preferred_element_type=jnp.float32)
    real_part = dot(left_re, right_re) - dot(left_im, right_im)
    imag_part = dot(left_re, right_im) + dot(left_im, right_re)
    return real_part.astype(jnp.bfloat16), imag_part.astype(jnp.bfloat16)


def exchange_kernel(
    n,
    flags,
    left_slot,
    extra_slot,
    is_extra,
    merges,
    finals,
    left_own,
    a_own,
    b_own,
    left_cross,
    a_cross,
    b_cross,
    out,
    lefts,
    a_full,
    b_full,
    left_plain,
    right_pair,
    left_relay,
    a_relay,
    b_relay,
    b_pick,
    panels,
    relayed,
    merged,
    left_sem,
    a_sem,
    b_sem,
    swap_sem,
    left_relay_sem,
    a_relay_sem,
    b_relay_sem,
    near_sem,
    relay_sem,
    far_sem,
    left_out_sem,
    a_out_sem,
    b_out_sem,
    swap_out_sem,
    left_cross_sem,
    a_cross_sem,
    b_cross_sem,
    left_pick_sem,
    a_pick_sem,
    b_pick_sem,
    near_out_sem,
    relay_out_sem,
    far_out_sem,
):
    me = lax.axis_index("node")
    parity = lax.rem(me, 2)
    partner = me + 1 - 2 * parity
    chunks, _, order, width = b_full.shape
    rows = left_own.shape[2]
    half, quarter = n // 2, n // 4
    extra = a_relay[0].shape[0]
    bands = len(left_relay)
    band = rows // bands
    tiles = order // TILE
    side, place = lax.div(me, half), lax.rem(me, half)
    own, other = side * half, (1 - side) * half
    lane, hop = lax.rem(me, quarter), lax.div(place, quarter)
    relays = quarter + side * (half - quarter)
    to_relay = half - side * (half - quarter) + lane
    is_relay = hop + side == 1

    barrier = pltpu.get_barrier_semaphore()

    @pl.loop(1, n)
    def _(t):
        pl.semaphore_signal(
            barrier,
            inc=1,
            device_id={"node": lax.rem(me + t, n)},
            device_id_type=pl.DeviceIdType.MESH,
        )

    pl.semaphore_wait(barrier, n - 1)

    def push(src, dst, send_sem, recv_sem, to):
        pltpu.make_async_remote_copy(
            src_ref=src,
            dst_ref=dst,
            send_sem=send_sem,
            recv_sem=recv_sem,
            device_id={"node": to},
            device_id_type=pl.DeviceIdType.MESH,
        ).start()

    def keep(src, dst, sem):
        pltpu.make_async_copy(src, dst, sem).start()

    def landed(ref, sem):
        pltpu.make_async_copy(ref, ref, sem).wait()

    def rows_of(device):
        return pl.ds(pl.multiple_of(device * rows, rows), rows)

    def band_of(device, r):
        return pl.ds(pl.multiple_of(device * rows + r * band, band), band)

    my_rows = rows_of(me)
    near, far = pl.ds(0, half), pl.ds(half, merged.shape[2])
    owners = [other + lane, other + quarter + lane]

    def others(step):
        @pl.loop(1, half)
        def _(t):
            step(lax.rem(place + t, half))

    for r in range(bands):
        push(
            left_cross.at[:, :, pl.ds(r * band, band)],
            left_relay[r].at[:, hop],
            left_cross_sem,
            left_relay_sem.at[r],
            to_relay,
        )

    others(
        lambda i: push(
            left_own.at[i], lefts.at[lax.rem(i, 2), :, my_rows], left_out_sem, left_sem, own + i
        )
    )
    keep(left_own.at[place], lefts.at[parity, :, my_rows], left_sem)

    for r in range(bands):
        push(
            a_cross.at[:, :, pl.ds(r * band, band)],
            a_relay[r].at[:, hop],
            a_cross_sem,
            a_relay_sem.at[r],
            to_relay,
        )

    others(lambda i: push(a_own.at[i], a_full.at[:, my_rows], a_out_sem, a_sem, own + i))
    keep(a_own.at[place], a_full.at[:, my_rows], a_sem)

    def push_right(c):
        push(
            b_cross.at[c], b_relay[c].at[:, hop], b_cross_sem.at[c], b_relay_sem.at[c], to_relay
        )
        others(
            lambda i: push(
                b_own.at[c, i], b_full.at[c, :, my_rows], b_out_sem.at[c], b_sem.at[c], own + i
            )
        )
        keep(b_own.at[c, place], b_full.at[c, :, my_rows], b_sem.at[c])

    for c in range(min(AHEAD, chunks)):
        push_right(c)

    for c in range(chunks):
        panels[c][half + merged.shape[2]] = jnp.zeros(panels[c].shape[1:], panels[c].dtype)
        relayed[c][half] = jnp.zeros(relayed[c].shape[1:], relayed[c].dtype)

    @pl.when(is_relay)
    def _():
        for r in range(bands):
            landed(left_relay[r], left_relay_sem.at[r])
            for j, owner in enumerate(owners):
                others(
                    lambda i: push(
                        left_relay[r].at[i, j],
                        lefts.at[lax.rem(i, 2), :, band_of(owner, r)],
                        left_pick_sem,
                        left_sem,
                        own + i,
                    )
                )
                keep(left_relay[r].at[place, j], lefts.at[parity, :, band_of(owner, r)], left_sem)

    landed(lefts.at[parity], left_sem)
    push(lefts.at[parity], lefts.at[parity], swap_out_sem, swap_sem, partner)
    landed(lefts.at[1 - parity], swap_sem)

    def block(i):
        return pl.ds(pl.multiple_of(i * TILE, TILE), TILE)

    @pl.loop(0, tiles * tiles)
    def _(t):
        down, across = block(lax.div(t, tiles)), block(lax.rem(t, tiles))
        real_part, imag_part = tile_product(
            lefts[0, 0, down, :], lefts[0, 1, down, :], lefts[1, 0, :, across], lefts[1, 1, :, across]
        )
        left_plain[0, down, across] = real_part
        left_plain[1, down, across] = imag_part

    landed(lefts.at[parity], swap_out_sem)
    left_used = lefts.at[0]
    flipped = flags[me] == 1

    @pl.loop(0, tiles * tiles)
    def _(t):
        down, across = block(lax.div(t, tiles)), block(lax.rem(t, tiles))
        left_used[0, down, across] = jnp.where(
            flipped, left_plain[0, across, down].T, left_plain[0, down, across]
        )
        left_used[1, down, across] = jnp.where(
            flipped, -left_plain[1, across, down].T, left_plain[1, down, across]
        )

    def pick_rows(i, j, r):
        return pl.ds(pl.multiple_of((2 * i + j) * rows + r * band, band), band)

    @pl.when(is_relay)
    def _():
        for r in range(bands):
            landed(a_relay[r], a_relay_sem.at[r])

            @pl.loop(0, half)
            def _(i):
                known = left_relay[r][2 * left_slot[own + i]]
                new = a_relay[r][extra_slot[own + i]]
                value = jnp.where(is_extra[own + i] == 1, new, known)
                for j in range(2):
                    left_plain[:, pick_rows(i, j, r), :] = value[j]

            for j, owner in enumerate(owners):
                others(
                    lambda i: push(
                        left_plain.at[:, pick_rows(i, j, r)],
                        a_full.at[:, band_of(owner, r)],
                        a_pick_sem,
                        a_sem,
                        own + i,
                    )
                )
                keep(left_plain.at[:, pick_rows(place, j, r)], a_full.at[:, band_of(owner, r)], a_sem)

    landed(a_full, a_sem)

    def relay_right(c):
        landed(b_relay[c], b_relay_sem.at[c])

        @pl.loop(0, half)
        def _(i):
            for r in range(bands):
                known = left_relay[r][
                    2 * left_slot[own + i] + 1, :, :, :, c * width : (c + 1) * width
                ]
                new = b_relay[c][extra_slot[own + i], :, :, r * band : (r + 1) * band, :]
                value = jnp.where(is_extra[own + i] == 1, new, known)
                b_pick[c, i, :, :, r * band : (r + 1) * band, :] = value

        for j, owner in enumerate(owners):
            others(
                lambda i: push(
                    b_pick.at[c, i, j],
                    b_full.at[c, :, rows_of(owner)],
                    b_pick_sem.at[c],
                    b_sem.at[c],
                    own + i,
                )
            )
            keep(b_pick.at[c, place, j], b_full.at[c, :, rows_of(owner)], b_sem.at[c])

    def compute(c):
        landed(b_full.at[c], b_sem.at[c])

        @pl.loop(0, tiles)
        def _(i):
            down = block(i)
            real_part, imag_part = tile_product(
                a_full[0, down, :], a_full[1, down, :], b_full[c, 0], b_full[c, 1]
            )
            right_pair[0, down, :] = real_part
            right_pair[1, down, :] = imag_part

        @pl.loop(0, tiles)
        def _(i):
            down = block(i)
            real_part, imag_part = tile_product(
                left_used[0, down, :], left_used[1, down, :], right_pair[0], right_pair[1]
            )
            b_full[c, 0, down, :] = real_part
            b_full[c, 1, down, :] = imag_part

        def to_far(q):
            for j in range(2):
                push(
                    b_full.at[c, :, rows_of(other + j * quarter + q)],
                    relayed[c].at[place, j],
                    relay_out_sem.at[c],
                    relay_sem.at[c],
                    relays + q,
                )

        @pl.loop(1, quarter)
        def _(t):
            to_far(lax.rem(lane + t, quarter))

        @pl.when(is_relay)
        def _():
            for j, owner in enumerate(owners):
                keep(b_full.at[c, :, rows_of(owner)], relayed[c].at[place, j], relay_sem.at[c])

        @pl.when(jnp.logical_not(is_relay))
        def _():
            to_far(lane)

        others(
            lambda i: push(
                b_full.at[c, :, rows_of(own + i)],
                panels[c].at[place],
                near_out_sem.at[c],
                near_sem.at[c],
                own + i,
            )
        )
        keep(b_full.at[c, :, my_rows], panels[c].at[place], near_sem.at[c])

    def merge(c):
        landed(relayed[c].at[near], relay_sem.at[c])

        @pl.loop(0, merged.shape[2])
        def _(t):
            at = 2 * (side * merged.shape[2] + t)
            first = relayed[c][merges[at]].astype(jnp.float32)
            second = relayed[c][merges[at + 1]].astype(jnp.float32)
            total = (first + second).astype(merged.dtype)
            for j in range(2):
                merged[c, j, t] = total[j]

        for j, owner in enumerate(owners):
            push(merged.at[c, j], panels[c].at[far], far_out_sem.at[c], far_sem.at[c], owner)

    for c in range(chunks):
        pl.when(is_relay)(functools.partial(relay_right, c))
        compute(c)
        if c + AHEAD < chunks:
            push_right(c + AHEAD)
        pl.when(is_relay)(functools.partial(merge, c))

    for c in range(chunks):
        landed(panels[c].at[near], near_sem.at[c])
        landed(panels[c].at[far], far_sem.at[c])

        @pl.loop(0, out.shape[0])
        def _(d):
            at = 2 * (side * out.shape[0] + d)
            first = panels[c][finals[at]].astype(jnp.float32)
            second = panels[c][finals[at + 1]].astype(jnp.float32)
            out[d, :, :, c * width : (c + 1) * width] = (first + second).astype(out.dtype)

    rest = pl.ds(0, half - 1)
    landed(left_cross, left_cross_sem)
    landed(left_own.at[rest], left_out_sem)
    landed(a_cross, a_cross_sem)
    landed(a_own.at[rest], a_out_sem)
    for c in range(chunks):
        landed(b_cross.at[c], b_cross_sem.at[c])
        landed(b_own.at[c, rest], b_out_sem.at[c])
        landed(panels[c].at[rest], near_out_sem.at[c])
        landed(relayed[c].at[pl.ds(0, quarter - 1)], relay_out_sem.at[c])

    @pl.when(is_relay)
    def _():
        for r in range(bands):
            landed(left_relay[r].at[rest], left_pick_sem)
            landed(left_relay[r].at[rest], a_pick_sem)
        for c in range(chunks):
            landed(b_pick.at[c, rest], b_pick_sem.at[c])
            landed(merged.at[c], far_out_sem.at[c])

    @pl.when(jnp.logical_not(is_relay))
    def _():
        for c in range(chunks):
            landed(relayed[c].at[0], relay_out_sem.at[c])


def local(nodes, pair_nodes, prod_left, prod_right, prod_flag, prod_diag, *, n):
    _, parts, rows, order = nodes.shape
    count = prod_left.shape[0]
    assert count == n == pair_nodes.shape[0] and rows * n == order and n % 4 == 0
    half = diags = count // 2
    extra, slots = plan_sizes(count)
    chunks = order // WIDTH
    width = order // chunks
    bands = rows // BAND
    sources = 2
    tables_and_rows = plan_and_gather(
        n, nodes, pair_nodes, prod_left, prod_right, prod_flag, prod_diag, chunks
    )
    kind = nodes.dtype
    dma = pltpu.SemaphoreType.DMA
    smem = pl.BlockSpec(memory_space=pltpu.SMEM)
    anywhere = pl.BlockSpec(memory_space=pl.ANY)
    return pl.pallas_call(
        functools.partial(exchange_kernel, n),
        out_shape=jax.ShapeDtypeStruct((diags, parts, rows, order), kind),
        in_specs=[smem] * 6 + [anywhere] * 6,
        out_specs=pl.BlockSpec(memory_space=pltpu.VMEM),
        scratch_shapes=[
            pltpu.VMEM((2, parts, order, order), kind),
            pltpu.VMEM((parts, order, order), kind),
            pltpu.VMEM((chunks, parts, order, width), kind),
            pltpu.VMEM((parts, order, order), kind),
            pltpu.VMEM((parts, order, width), kind),
            [pltpu.VMEM((half, sources, parts, BAND, order), kind)] * bands,
            [pltpu.VMEM((extra, sources, parts, BAND, order), kind)] * bands,
            [pltpu.VMEM((extra, sources, parts, rows, width), kind)] * chunks,
            pltpu.VMEM((chunks, half, sources, parts, rows, width), kind),
            [pltpu.VMEM((half + slots + 1, parts, rows, width), kind)] * chunks,
            [pltpu.VMEM((half + 1, sources, parts, rows, width), kind)] * chunks,
            pltpu.VMEM((chunks, sources, slots, parts, rows, width), kind),
            dma,
            dma,
            dma((chunks,)),
            dma,
            dma((bands,)),
            dma((bands,)),
            dma((chunks,)),
            dma((chunks,)),
            dma((chunks,)),
            dma((chunks,)),
            dma,
            dma,
            dma((chunks,)),
            dma,
            dma,
            dma,
            dma((chunks,)),
            dma,
            dma,
            dma((chunks,)),
            dma((chunks,)),
            dma((chunks,)),
            dma((chunks,)),
        ],
        compiler_params=pltpu.CompilerParams(
            collective_id=0, has_side_effects=True, vmem_limit_bytes=51 * 2**20
        ),
    )(*tables_and_rows)


def solution(mesh):
    placed = (P("grp", None, "node", None), P(), P(), P(), P(), P())
    return jax.shard_map(
        functools.partial(local, n=mesh.shape["node"]),
        mesh=mesh,
        in_specs=placed,
        out_specs=P("grp", None, "node", None),
        check_vma=False,
    )
```

time: 346 us -> 440 us (1.27)
  Pallas kernels: 343 us -> 426 us
  local copies, waits for them, and re-layouts: 2.8 us -> 11.1 us
    pallas_call x1, Pallas kernels: 336 us -> 419 us  [local(): pl.pallas_call(functools.partial(exchange_kernel, n), out_shape=jax.Shape...]
    unnamed x1 -> x11, local copies, waits for them, and re-layouts: 1.32 us -> 9.65 us
where the time goes in v1:
time: 440 us; the launch traced here: 437 us
  Pallas kernels  426 us (97%)
  local copies, waits for them, and re-layouts  11.1 us (3%)
    pallas_call x1, Pallas kernels, local(): pl.pallas_call(functools.partial(exchange_kernel, n), out_shape=jax.Shape...  419 us
    unnamed x11, local copies, waits for them, and re-layouts  9.65 us

profile of v1, /device:TPU:13, one launch (start us, length us, event | category | flops | bytes accessed | tf_op | source)
XLA Modules:
  0.0 437.4 jit_solution(8689174531029270481)
XLA Ops:
  0.0 0.8 slice_bitcast_fusion
  0.8 0.7 stack.19.graph
  1.5 7.2 %shard_map.64 = (s32[16]{0:T(128)S(1)}, s32[16]{0:T(128)S(1)}, s32[16]{0:T(128)S(1)}, s32[16]{0:T(128)S(1)}, s32[24]{0:T(128)S(1)}, /*index=5*/s32[32]{0:T(128)S...) custom-call(s32[6,16]{1,0:T(8,128)S(1)} %stack.19.graph, ...), custom_call_target="tpu_custom_call" | custom-call | tf_op jit(solution)/shard_map/pallas_call | solution.py:254
  8.7 0.0 copy-start
  8.7 1.3 copy-done
  10.0 0.0 copy-start.1
  10.0 1.4 copy-done.1
  11.3 0.0 copy-start.2
  11.3 1.3 copy-done.2
  12.6 0.0 copy-start.3
  12.7 1.3 copy-done.3
  14.0 0.0 copy-start.4
  14.0 1.2 copy-done.4
  15.2 419.1 %shard_map.65 = bf16[8,2,64,1024]{3,2,1,0:T(8,128)(2,1)} custom-call(s32[16]{0:T(128)S(1)} %get-tuple-element.17.flags, s32[16]{0:T(128)S(1)} %get-tuple-element.18.left_slot, s32[16]{0:T(128)S(1)} %get-tuple-element.19.extra_slot, s32[16]{0:T(128)S(1)} %get-tuple-element.20.is_extra, s32[24]{0:T(128)S(1)} %get-tuple-element.21.merges, ...), custom_call_target="tpu_custom_call" | custom-call | tf_op jit(solution)/shard_map/pallas_call | solution.py:687
  434.3 3.1 copy.8
Async XLA Ops:
  8.7 1.3 copy-start
  10.0 1.4 copy-start.1
  11.3 1.3 copy-start.2
  12.6 1.3 copy-start.3
  14.0 1.2 copy-start.4

commit v2 on v1

--- a/solution.py
+++ b/solution.py
@@ -8,7 +8,6 @@
 from jax.sharding import PartitionSpec as P
 
 TILE = 256
-AHEAD = 8
 WIDTH = 128
 BAND = 16
 LANES = 128
@@ -320,7 +319,6 @@
     b_pick,
     panels,
     relayed,
-    merged,
     left_sem,
     a_sem,
     b_sem,
@@ -351,8 +349,8 @@
     chunks, _, order, width = b_full.shape
     rows = left_own.shape[2]
     half, quarter = n // 2, n // 4
-    extra = a_relay[0].shape[0]
-    bands = len(left_relay)
+    extra = a_relay[0][0].shape[0]
+    bands = len(left_relay[0])
     band = rows // bands
     tiles = order // TILE
     side, place = lax.div(me, half), lax.rem(me, half)
@@ -398,46 +396,51 @@
         return pl.ds(pl.multiple_of(device * rows + r * band, band), band)
 
     my_rows = rows_of(me)
-    near, far = pl.ds(0, half), pl.ds(half, merged.shape[2])
+    slots = merges.shape[0] // 4
+    near, far = pl.ds(0, half), pl.ds(half, slots)
     owners = [other + lane, other + quarter + lane]
+    senders = [other + (1 - side) * quarter + lane, other + side * quarter + lane]
+
+    def by_role(step):
+        pl.when(jnp.logical_not(is_relay))(functools.partial(step, 0))
+        pl.when(is_relay)(functools.partial(step, 1))
 
     def others(step):
         @pl.loop(1, half)
         def _(t):
             step(lax.rem(place + t, half))
 
-    for r in range(bands):
-        push(
-            left_cross.at[:, :, pl.ds(r * band, band)],
-            left_relay[r].at[:, hop],
-            left_cross_sem,
-            left_relay_sem.at[r],
-            to_relay,
-        )
-
-    others(
-        lambda i: push(
-            left_own.at[i], lefts.at[lax.rem(i, 2), :, my_rows], left_out_sem, left_sem, own + i
-        )
-    )
-    keep(left_own.at[place], lefts.at[parity, :, my_rows], left_sem)
-
-    for r in range(bands):
-        push(
-            a_cross.at[:, :, pl.ds(r * band, band)],
-            a_relay[r].at[:, hop],
-            a_cross_sem,
-            a_relay_sem.at[r],
-            to_relay,
-        )
-
-    others(lambda i: push(a_own.at[i], a_full.at[:, my_rows], a_out_sem, a_sem, own + i))
-    keep(a_own.at[place], a_full.at[:, my_rows], a_sem)
-
-    def push_right(c):
-        push(
-            b_cross.at[c], b_relay[c].at[:, hop], b_cross_sem.at[c], b_relay_sem.at[c], to_relay
-        )
+    def cross_left(role):
+        for r in range(bands):
+            push(
+                left_cross.at[:, :, pl.ds(r * band, band)],
+                left_relay[role][r],
+                left_cross_sem,
+                left_relay_sem.at[role, r],
+                to_relay,
+            )
+
+    def cross_a(role):
+        for r in range(bands):
+            push(
+                a_cross.at[:, :, pl.ds(r * band, band)],
+                a_relay[role][r],
+                a_cross_sem,
+                a_relay_sem.at[role, r],
+                to_relay,
+            )
+
+    def cross_b(role):
+        for c in range(chunks):
+            push(
+                b_cross.at[c],
+                b_relay[c].at[pl.ds(0, extra), role],
+                b_cross_sem.at[c],
+                b_relay_sem.at[c],
+                to_relay,
+            )
+
+    def share_b(c):
         others(
             lambda i: push(
                 b_own.at[c, i], b_full.at[c, :, my_rows], b_out_sem.at[c], b_sem.at[c], own + i
@@ -445,30 +448,62 @@
         )
         keep(b_own.at[c, place], b_full.at[c, :, my_rows], b_sem.at[c])
 
-    for c in range(min(AHEAD, chunks)):
-        push_right(c)
+    def share_left():
+        others(
+            lambda i: push(
+                left_own.at[i],
+                lefts.at[lax.rem(i, 2), :, my_rows],
+                left_out_sem,
+                left_sem,
+                own + i,
+            )
+        )
+        keep(left_own.at[place], lefts.at[parity, :, my_rows], left_sem)
+
+    def share_a():
+        others(lambda i: push(a_own.at[i], a_full.at[:, my_rows], a_out_sem, a_sem, own + i))
+        keep(a_own.at[place], a_full.at[:, my_rows], a_sem)
+
+    by_role(cross_left)
+    share_left()
+    share_a()
+    by_role(cross_a)
+
+    @pl.when(jnp.logical_not(is_relay))
+    def _():
+        for c in range(chunks):
+            share_b(c)
+
+    pl.when(is_relay)(functools.partial(cross_b, 1))
 
     for c in range(chunks):
-        panels[c][half + merged.shape[2]] = jnp.zeros(panels[c].shape[1:], panels[c].dtype)
+        panels[c][half + slots] = jnp.zeros(panels[c].shape[1:], panels[c].dtype)
         relayed[c][half] = jnp.zeros(relayed[c].shape[1:], relayed[c].dtype)
 
     @pl.when(is_relay)
     def _():
-        for r in range(bands):
-            landed(left_relay[r], left_relay_sem.at[r])
-            for j, owner in enumerate(owners):
+        for role, sender in enumerate(senders):
+            for r in range(bands):
+                landed(left_relay[role][r], left_relay_sem.at[role, r])
                 others(
                     lambda i: push(
-                        left_relay[r].at[i, j],
-                        lefts.at[lax.rem(i, 2), :, band_of(owner, r)],
+                        left_relay[role][r].at[i],
+                        lefts.at[lax.rem(i, 2), :, band_of(sender, r)],
                         left_pick_sem,
                         left_sem,
                         own + i,
                     )
                 )
-                keep(left_relay[r].at[place, j], lefts.at[parity, :, band_of(owner, r)], left_sem)
+                keep(
+                    left_relay[role][r].at[place],
+                    lefts.at[parity, :, band_of(sender, r)],
+                    left_sem,
+                )
+        for c in range(chunks):
+            share_b(c)
 
     landed(lefts.at[parity], left_sem)
+
     push(lefts.at[parity], lefts.at[parity], swap_out_sem, swap_sem, partner)
     landed(lefts.at[1 - parity], swap_sem)
 
@@ -498,60 +533,65 @@
             flipped, -left_plain[1, across, down].T, left_plain[1, down, across]
         )
 
-    def pick_rows(i, j, r):
-        return pl.ds(pl.multiple_of((2 * i + j) * rows + r * band, band), band)
+    def pick_rows(i, role, r):
+        return pl.ds(pl.multiple_of((2 * i + role) * rows + r * band, band), band)
 
     @pl.when(is_relay)
     def _():
-        for r in range(bands):
-            landed(a_relay[r], a_relay_sem.at[r])
-
-            @pl.loop(0, half)
-            def _(i):
-                known = left_relay[r][2 * left_slot[own + i]]
-                new = a_relay[r][extra_slot[own + i]]
-                value = jnp.where(is_extra[own + i] == 1, new, known)
-                for j in range(2):
-                    left_plain[:, pick_rows(i, j, r), :] = value[j]
-
-            for j, owner in enumerate(owners):
+        for role, sender in enumerate(senders):
+            for r in range(bands):
+                landed(a_relay[role][r], a_relay_sem.at[role, r])
+
+                @pl.loop(0, half)
+                def _(i):
+                    known = left_relay[role][r][2 * left_slot[own + i]]
+                    new = a_relay[role][r][extra_slot[own + i]]
+                    left_plain[:, pick_rows(i, role, r), :] = jnp.where(
+                        is_extra[own + i] == 1, new, known
+                    )
+
                 others(
                     lambda i: push(
-                        left_plain.at[:, pick_rows(i, j, r)],
-                        a_full.at[:, band_of(owner, r)],
+                        left_plain.at[:, pick_rows(i, role, r)],
+                        a_full.at[:, band_of(sender, r)],
                         a_pick_sem,
                         a_sem,
                         own + i,
                     )
                 )
-                keep(left_plain.at[:, pick_rows(place, j, r)], a_full.at[:, band_of(owner, r)], a_sem)
+                keep(
+                    left_plain.at[:, pick_rows(place, role, r)],
+                    a_full.at[:, band_of(sender, r)],
+                    a_sem,
+                )
 
     landed(a_full, a_sem)
+    pl.when(jnp.logical_not(is_relay))(functools.partial(cross_b, 0))
 
     def relay_right(c):
-        landed(b_relay[c], b_relay_sem.at[c])
+        landed(b_relay[c].at[pl.ds(0, extra)], b_relay_sem.at[c])
+        across = pl.ds(c * width, width)
 
         @pl.loop(0, half)
         def _(i):
-            for r in range(bands):
-                known = left_relay[r][
-                    2 * left_slot[own + i] + 1, :, :, :, c * width : (c + 1) * width
-                ]
-                new = b_relay[c][extra_slot[own + i], :, :, r * band : (r + 1) * band, :]
-                value = jnp.where(is_extra[own + i] == 1, new, known)
-                b_pick[c, i, :, :, r * band : (r + 1) * band, :] = value
-
-        for j, owner in enumerate(owners):
+            for role in range(2):
+                for r in range(bands):
+                    down = pl.ds(r * band, band)
+                    known = left_relay[role][r][2 * left_slot[own + i] + 1, :, :, across]
+                    new = b_relay[c][extra_slot[own + i], role, :, down, :]
+                    b_pick[c, i, role, :, down, :] = jnp.where(is_extra[own + i] == 1, new, known)
+
+        for role, sender in enumerate(senders):
             others(
                 lambda i: push(
-                    b_pick.at[c, i, j],
-                    b_full.at[c, :, rows_of(owner)],
+                    b_pick.at[c, i, role],
+                    b_full.at[c, :, rows_of(sender)],
                     b_pick_sem.at[c],
                     b_sem.at[c],
                     own + i,
                 )
             )
-            keep(b_pick.at[c, place, j], b_full.at[c, :, rows_of(owner)], b_sem.at[c])
+            keep(b_pick.at[c, place, role], b_full.at[c, :, rows_of(sender)], b_sem.at[c])
 
     def compute(c):
         landed(b_full.at[c], b_sem.at[c])
@@ -611,24 +651,30 @@
     def merge(c):
         landed(relayed[c].at[near], relay_sem.at[c])
 
-        @pl.loop(0, merged.shape[2])
+        @pl.loop(0, slots)
         def _(t):
-            at = 2 * (side * merged.shape[2] + t)
+            at = 2 * (side * slots + t)
             first = relayed[c][merges[at]].astype(jnp.float32)
             second = relayed[c][merges[at + 1]].astype(jnp.float32)
-            total = (first + second).astype(merged.dtype)
-            for j in range(2):
-                merged[c, j, t] = total[j]
+            b_relay[c][t] = (first + second).astype(out.dtype)
 
         for j, owner in enumerate(owners):
-            push(merged.at[c, j], panels[c].at[far], far_out_sem.at[c], far_sem.at[c], owner)
-
+            push(
+                b_relay[c].at[pl.ds(0, slots), j],
+                panels[c].at[far],
+                far_out_sem.at[c],
+                far_sem.at[c],
+                owner,
+            )
+
+    pl.when(is_relay)(functools.partial(relay_right, 0))
     for c in range(chunks):
-        pl.when(is_relay)(functools.partial(relay_right, c))
+        if c + 1 < chunks:
+            pl.when(is_relay)(functools.partial(relay_right, c + 1))
         compute(c)
-        if c + AHEAD < chunks:
-            push_right(c + AHEAD)
-        pl.when(is_relay)(functools.partial(merge, c))
+        if c > 0:
+            pl.when(is_relay)(functools.partial(merge, c - 1))
+    pl.when(is_relay)(functools.partial(merge, chunks - 1))
 
     for c in range(chunks):
         landed(panels[c].at[near], near_sem.at[c])
@@ -654,12 +700,13 @@
 
     @pl.when(is_relay)
     def _():
-        for r in range(bands):
-            landed(left_relay[r].at[rest], left_pick_sem)
-            landed(left_relay[r].at[rest], a_pick_sem)
+        for role in range(2):
+            for r in range(bands):
+                landed(left_relay[role][r].at[rest], left_pick_sem)
+                landed(left_relay[role][r].at[rest], a_pick_sem)
         for c in range(chunks):
             landed(b_pick.at[c, rest], b_pick_sem.at[c])
-            landed(merged.at[c], far_out_sem.at[c])
+            landed(b_relay[c].at[pl.ds(0, slots)], far_out_sem.at[c])
 
     @pl.when(jnp.logical_not(is_relay))
     def _():
@@ -681,6 +728,9 @@
         n, nodes, pair_nodes, prod_left, prod_right, prod_flag, prod_diag, chunks
     )
     kind = nodes.dtype
+    matrix = parts * order * order
+    blocks = 4 * half + 2 * extra + 2 * max(extra, slots) + (half + slots + 1) + 2 * (half + 1)
+    held = 5 * matrix + parts * order * width + blocks * parts * rows * order
     dma = pltpu.SemaphoreType.DMA
     smem = pl.BlockSpec(memory_space=pltpu.SMEM)
     anywhere = pl.BlockSpec(memory_space=pl.ANY)
@@ -695,19 +745,18 @@
             pltpu.VMEM((chunks, parts, order, width), kind),
             pltpu.VMEM((parts, order, order), kind),
             pltpu.VMEM((parts, order, width), kind),
-            [pltpu.VMEM((half, sources, parts, BAND, order), kind)] * bands,
-            [pltpu.VMEM((extra, sources, parts, BAND, order), kind)] * bands,
-            [pltpu.VMEM((extra, sources, parts, rows, width), kind)] * chunks,
+            [[pltpu.VMEM((half, parts, BAND, order), kind)] * bands] * sources,
+            [[pltpu.VMEM((extra, parts, BAND, order), kind)] * bands] * sources,
+            [pltpu.VMEM((max(extra, slots), sources, parts, rows, width), kind)] * chunks,
             pltpu.VMEM((chunks, half, sources, parts, rows, width), kind),
             [pltpu.VMEM((half + slots + 1, parts, rows, width), kind)] * chunks,
             [pltpu.VMEM((half + 1, sources, parts, rows, width), kind)] * chunks,
-            pltpu.VMEM((chunks, sources, slots, parts, rows, width), kind),
-            dma,
-            dma,
-            dma((chunks,)),
-            dma,
-            dma((bands,)),
-            dma((bands,)),
+            dma,
+            dma,
+            dma((chunks,)),
+            dma,
+            dma((sources, bands)),
+            dma((sources, bands)),
             dma((chunks,)),
             dma((chunks,)),
             dma((chunks,)),
@@ -727,7 +776,7 @@
             dma((chunks,)),
         ],
         compiler_params=pltpu.CompilerParams(
-            collective_id=0, has_side_effects=True, vmem_limit_bytes=51 * 2**20
+            collective_id=0, has_side_effects=True, vmem_limit_bytes=held * kind.itemsize + 2**20
         ),
     )(*tables_and_rows)
 

time: 440 us -> 328 us (0.75)
  Pallas kernels: 426 us -> 322 us
  local copies, waits for them, and re-layouts: 11.1 us -> 5.44 us
    pallas_call x1, Pallas kernels: 419 us -> 315 us  [local(): pl.pallas_call(functools.partial(exchange_kernel, n), out_shape=jax.Shape...]
    unnamed x11 -> x5, local copies, waits for them, and re-layouts: 9.65 us -> 3.97 us
where the time goes in v2:
time: 328 us
  Pallas kernels  322 us (98%)
  local copies, waits for them, and re-layouts  5.44 us (2%)
    pallas_call x1, Pallas kernels, local(): pl.pallas_call(functools.partial(exchange_kernel, n), out_shape=jax.Shape...  315 us
    pallas_call x1, Pallas kernels, plan_and_gather(): pl.pallas_call(functools.partial(plan_and_gather_kernel, n), out_shape=(t...  7.07 us

profile of v2, /device:TPU:13, one launch (start us, length us, event | category | flops | bytes accessed | tf_op | source)
XLA Modules:
  0.0 327.5 jit_solution(7204494290201053888)
XLA Ops:
  0.0 0.8 slice_bitcast_fusion
  0.8 0.7 stack.19.graph
  1.5 7.1 %shard_map.64 = (s32[16]{0:T(128)S(1)}, s32[16]{0:T(128)S(1)}, s32[16]{0:T(128)S(1)}, s32[16]{0:T(128)S(1)}, s32[24]{0:T(128)S(1)}, /*index=5*/s32[32]{0:T(128)S...) custom-call(s32[6,16]{1,0:T(8,128)S(1)} %stack.19.graph, ...), custom_call_target="tpu_custom_call" | custom-call | tf_op jit(solution)/shard_map/pallas_call | solution.py:253
  8.6 0.0 copy-start
  8.6 1.3 copy-done
  9.9 0.0 copy-start.1
  9.9 1.3 copy-done.1
  11.2 315.0 %shard_map.65 = bf16[8,2,64,1024]{3,2,1,0:T(8,128)(2,1)S(1)} custom-call(s32[16]{0:T(128)S(1)} %get-tuple-element.17.flags, s32[16]{0:T(128)S(1)} %get-tuple-element.18.left_slot, s32[16]{0:T(128)S(1)} %get-tuple-element.19.extra_slot, s32[16]{0:T(128)S(1)} %get-tuple-element.20.is_extra, s32[24]{0:T(128)S(1)} %get-tuple-element.21.merges, ...), custom_call_target="tpu_custom_call" | custom-call | tf_op jit(solution)/shard_map/pallas_call | solution.py:737
  326.2 1.3 copy.8
Async XLA Ops:
  8.6 1.3 copy-start
  9.9 1.3 copy-start.1

commit v3 on v2

--- a/solution.py
+++ b/solution.py
@@ -9,6 +9,8 @@
 
 TILE = 256
 WIDTH = 128
+EARLY = 3
+AHEAD = 3
 BAND = 16
 LANES = 128
 
@@ -54,16 +56,18 @@
     own = jnp.maximum(own_0, own_1)
     bad = jnp.where(ones != groups // 2, 4096.0, 0.0)
     bad = bad + jnp.where(new > extra, 256.0, 0.0) + jnp.where(own > slots, 256.0, 0.0)
-    cost = bad + 2 * new + own
+    cost = bad + jnp.where(new > extra - 1, 64.0, 0.0) + 2 * new + own
     best = jnp.min(cost)
     index = lax.broadcasted_iota(jnp.int32, cost.shape, 1).astype(jnp.float32)
-    return jnp.min(jnp.where(cost == best, index, 1e9)).astype(jnp.int32)
+    mask = jnp.min(jnp.where(cost == best, index, 1e9)).astype(jnp.int32)
+    return mask, (best < 64.0).astype(jnp.int32)
 
 
 def plan_and_gather_kernel(
     n,
     graph,
     nodes,
+    small,
     flags,
     left_slot,
     extra_slot,
@@ -133,9 +137,9 @@
     lax.fori_loop(0, count, read, jnp.int32(0))
 
     if not searched(count):
-        mask = jnp.int32(2 ** (groups // 2) - 1)
+        mask, small[0] = jnp.int32(2 ** (groups // 2) - 1), 0
     else:
-        mask = choose_sides(graph, product, home, sides, group_of, extra, slots)
+        mask, small[0] = choose_sides(graph, product, home, sides, group_of, extra, slots)
 
     def place(g, counts):
         which = lax.rem(lax.shift_right_logical(mask, g), 2)
@@ -253,6 +257,7 @@
     return pl.pallas_call(
         functools.partial(plan_and_gather_kernel, n),
         out_shape=(
+            table(1),
             table(count),
             table(count),
             table(count),
@@ -267,7 +272,7 @@
             cut(extra),
         ),
         in_specs=[smem, pl.BlockSpec(memory_space=pltpu.HBM)],
-        out_specs=[smem] * 6 + [pl.BlockSpec(memory_space=pltpu.VMEM)] * 6,
+        out_specs=[smem] * 7 + [pl.BlockSpec(memory_space=pltpu.VMEM)] * 6,
         scratch_shapes=[
             scratch(2 * count),
             scratch(count),
@@ -282,7 +287,7 @@
             pltpu.SemaphoreType.DMA,
             pltpu.SemaphoreType.DMA,
         ],
-        compiler_params=pltpu.CompilerParams(vmem_limit_bytes=36 * 2**20),
+        compiler_params=pltpu.CompilerParams(vmem_limit_bytes=50 * 2**20),
     )(graph, nodes)
 
 
@@ -423,22 +428,21 @@
     def cross_a(role):
         for r in range(bands):
             push(
-                a_cross.at[:, :, pl.ds(r * band, band)],
+                a_cross.at[pl.ds(0, extra), :, pl.ds(r * band, band)],
                 a_relay[role][r],
                 a_cross_sem,
                 a_relay_sem.at[role, r],
                 to_relay,
             )
 
-    def cross_b(role):
-        for c in range(chunks):
-            push(
-                b_cross.at[c],
-                b_relay[c].at[pl.ds(0, extra), role],
-                b_cross_sem.at[c],
-                b_relay_sem.at[c],
-                to_relay,
-            )
+    def cross_b(role, c):
+        push(
+            b_cross.at[c, pl.ds(0, extra)],
+            b_relay[role][c].at[pl.ds(0, extra)],
+            b_cross_sem.at[c],
+            b_relay_sem.at[role, c],
+            to_relay,
+        )
 
     def share_b(c):
         others(
@@ -461,8 +465,12 @@
         keep(left_own.at[place], lefts.at[parity, :, my_rows], left_sem)
 
     def share_a():
-        others(lambda i: push(a_own.at[i], a_full.at[:, my_rows], a_out_sem, a_sem, own + i))
-        keep(a_own.at[place], a_full.at[:, my_rows], a_sem)
+        others(
+            lambda i: push(
+                a_own.at[i], a_full.at[:, my_rows], a_out_sem, a_sem.at[2 * bands], own + i
+            )
+        )
+        keep(a_own.at[place], a_full.at[:, my_rows], a_sem.at[2 * bands])
 
     by_role(cross_left)
     share_left()
@@ -474,7 +482,8 @@
         for c in range(chunks):
             share_b(c)
 
-    pl.when(is_relay)(functools.partial(cross_b, 1))
+    for c in range(chunks):
+        pl.when(is_relay)(functools.partial(cross_b, 1, c))
 
     for c in range(chunks):
         panels[c][half + slots] = jnp.zeros(panels[c].shape[1:], panels[c].dtype)
@@ -555,47 +564,56 @@
                         left_plain.at[:, pick_rows(i, role, r)],
                         a_full.at[:, band_of(sender, r)],
                         a_pick_sem,
-                        a_sem,
+                        a_sem.at[role * bands + r],
                         own + i,
                     )
                 )
                 keep(
                     left_plain.at[:, pick_rows(place, role, r)],
                     a_full.at[:, band_of(sender, r)],
-                    a_sem,
+                    a_sem.at[role * bands + r],
                 )
 
-    landed(a_full, a_sem)
-    pl.when(jnp.logical_not(is_relay))(functools.partial(cross_b, 0))
-
-    def relay_right(c):
-        landed(b_relay[c].at[pl.ds(0, extra)], b_relay_sem.at[c])
+    landed(a_full.at[:, pl.ds(0, quarter * band)], a_sem.at[max(2 * bands - 2, 0)])
+    for c in range(min(AHEAD, chunks)):
+        pl.when(jnp.logical_not(is_relay))(functools.partial(cross_b, 0, c))
+
+    def relay_right(role, c):
+        landed(b_relay[role][c].at[pl.ds(0, extra)], b_relay_sem.at[role, c])
         across = pl.ds(c * width, width)
 
         @pl.loop(0, half)
         def _(i):
-            for role in range(2):
-                for r in range(bands):
-                    down = pl.ds(r * band, band)
-                    known = left_relay[role][r][2 * left_slot[own + i] + 1, :, :, across]
-                    new = b_relay[c][extra_slot[own + i], role, :, down, :]
-                    b_pick[c, i, role, :, down, :] = jnp.where(is_extra[own + i] == 1, new, known)
-
-        for role, sender in enumerate(senders):
-            others(
-                lambda i: push(
-                    b_pick.at[c, i, role],
-                    b_full.at[c, :, rows_of(sender)],
-                    b_pick_sem.at[c],
-                    b_sem.at[c],
-                    own + i,
-                )
-            )
-            keep(b_pick.at[c, place, role], b_full.at[c, :, rows_of(sender)], b_sem.at[c])
+            for r in range(bands):
+                down = pl.ds(r * band, band)
+                known = left_relay[role][r][2 * left_slot[own + i] + 1, :, :, across]
+                new = b_relay[role][c][extra_slot[own + i], :, down, :]
+                b_pick[c, i, role, :, down, :] = jnp.where(is_extra[own + i] == 1, new, known)
+
+        others(
+            lambda i: push(
+                b_pick.at[c, i, role],
+                b_full.at[c, :, rows_of(senders[role])],
+                b_pick_sem.at[c],
+                b_sem.at[c],
+                own + i,
+            )
+        )
+        keep(
+            b_pick.at[c, place, role], b_full.at[c, :, rows_of(senders[role])], b_sem.at[c]
+        )
+
+    @pl.when(is_relay)
+    def _():
+        for c in range(min(EARLY, chunks)):
+            relay_right(1, c)
+
+    landed(a_full.at[:, pl.ds(0, half * rows)], a_sem.at[2 * bands])
+    for t in range(2 * bands):
+        if t != 2 * bands - 2:
+            landed(a_full.at[:, pl.ds(0, quarter * band)], a_sem.at[t])
 
     def compute(c):
-        landed(b_full.at[c], b_sem.at[c])
-
         @pl.loop(0, tiles)
         def _(i):
             down = block(i)
@@ -604,15 +622,6 @@
             )
             right_pair[0, down, :] = real_part
             right_pair[1, down, :] = imag_part
-
-        @pl.loop(0, tiles)
-        def _(i):
-            down = block(i)
-            real_part, imag_part = tile_product(
-                left_used[0, down, :], left_used[1, down, :], right_pair[0], right_pair[1]
-            )
-            b_full[c, 0, down, :] = real_part
-            b_full[c, 1, down, :] = imag_part
 
         def to_far(q):
             for j in range(2):
@@ -624,18 +633,32 @@
                     relays + q,
                 )
 
-        @pl.loop(1, quarter)
-        def _(t):
-            to_far(lax.rem(lane + t, quarter))
-
-        @pl.when(is_relay)
-        def _():
-            for j, owner in enumerate(owners):
-                keep(b_full.at[c, :, rows_of(owner)], relayed[c].at[place, j], relay_sem.at[c])
-
-        @pl.when(jnp.logical_not(is_relay))
-        def _():
-            to_far(lane)
+        def all_far():
+            @pl.loop(1, quarter)
+            def _(t):
+                to_far(lax.rem(lane + t, quarter))
+
+            @pl.when(is_relay)
+            def _():
+                for j, owner in enumerate(owners):
+                    keep(b_full.at[c, :, rows_of(owner)], relayed[c].at[place, j], relay_sem.at[c])
+
+            @pl.when(jnp.logical_not(is_relay))
+            def _():
+                to_far(lane)
+
+        piece = min(TILE, order // 2)
+
+        @pl.loop(0, order // piece)
+        def _(i):
+            start = lax.rem(other * rows + i * piece, order)
+            down = pl.ds(pl.multiple_of(start, piece), piece)
+            real_part, imag_part = tile_product(
+                left_used[0, down, :], left_used[1, down, :], right_pair[0], right_pair[1]
+            )
+            b_full[c, 0, down, :] = real_part
+            b_full[c, 1, down, :] = imag_part
+            pl.when(i == order // piece // 2 - 1)(all_far)
 
         others(
             lambda i: push(
@@ -656,21 +679,28 @@
             at = 2 * (side * slots + t)
             first = relayed[c][merges[at]].astype(jnp.float32)
             second = relayed[c][merges[at + 1]].astype(jnp.float32)
-            b_relay[c][t] = (first + second).astype(out.dtype)
+            total = (first + second).astype(out.dtype)
+            for j in range(2):
+                b_relay[j][c][t] = total[j]
 
         for j, owner in enumerate(owners):
             push(
-                b_relay[c].at[pl.ds(0, slots), j],
+                b_relay[j][c].at[pl.ds(0, slots)],
                 panels[c].at[far],
                 far_out_sem.at[c],
                 far_sem.at[c],
                 owner,
             )
 
-    pl.when(is_relay)(functools.partial(relay_right, 0))
+    pl.when(is_relay)(functools.partial(relay_right, 0, 0))
     for c in range(chunks):
         if c + 1 < chunks:
-            pl.when(is_relay)(functools.partial(relay_right, c + 1))
+            pl.when(is_relay)(functools.partial(relay_right, 0, c + 1))
+        if c + EARLY < chunks:
+            pl.when(is_relay)(functools.partial(relay_right, 1, c + EARLY))
+        landed(b_full.at[c], b_sem.at[c])
+        if c + AHEAD < chunks:
+            pl.when(jnp.logical_not(is_relay))(functools.partial(cross_b, 0, c + AHEAD))
         compute(c)
         if c > 0:
             pl.when(is_relay)(functools.partial(merge, c - 1))
@@ -690,10 +720,10 @@
     rest = pl.ds(0, half - 1)
     landed(left_cross, left_cross_sem)
     landed(left_own.at[rest], left_out_sem)
-    landed(a_cross, a_cross_sem)
+    landed(a_cross.at[pl.ds(0, extra)], a_cross_sem)
     landed(a_own.at[rest], a_out_sem)
     for c in range(chunks):
-        landed(b_cross.at[c], b_cross_sem.at[c])
+        landed(b_cross.at[c, pl.ds(0, extra)], b_cross_sem.at[c])
         landed(b_own.at[c, rest], b_out_sem.at[c])
         landed(panels[c].at[rest], near_out_sem.at[c])
         landed(relayed[c].at[pl.ds(0, quarter - 1)], relay_out_sem.at[c])
@@ -706,7 +736,8 @@
                 landed(left_relay[role][r].at[rest], a_pick_sem)
         for c in range(chunks):
             landed(b_pick.at[c, rest], b_pick_sem.at[c])
-            landed(b_relay[c].at[pl.ds(0, slots)], far_out_sem.at[c])
+            for j in range(2):
+                landed(b_relay[j][c].at[pl.ds(0, slots)], far_out_sem.at[c])
 
     @pl.when(jnp.logical_not(is_relay))
     def _():
@@ -714,20 +745,14 @@
             landed(relayed[c].at[0], relay_out_sem.at[c])
 
 
-def local(nodes, pair_nodes, prod_left, prod_right, prod_flag, prod_diag, *, n):
-    _, parts, rows, order = nodes.shape
-    count = prod_left.shape[0]
-    assert count == n == pair_nodes.shape[0] and rows * n == order and n % 4 == 0
-    half = diags = count // 2
-    extra, slots = plan_sizes(count)
-    chunks = order // WIDTH
-    width = order // chunks
+def exchange(n, rows_in, extra, which):
+    *_, merges, _, left_own, _, b_own, _, _, _ = rows_in
+    half, parts, rows, order = left_own.shape
+    chunks, width = b_own.shape[0], b_own.shape[-1]
+    slots = merges.shape[0] // 4
     bands = rows // BAND
     sources = 2
-    tables_and_rows = plan_and_gather(
-        n, nodes, pair_nodes, prod_left, prod_right, prod_flag, prod_diag, chunks
-    )
-    kind = nodes.dtype
+    kind = left_own.dtype
     matrix = parts * order * order
     blocks = 4 * half + 2 * extra + 2 * max(extra, slots) + (half + slots + 1) + 2 * (half + 1)
     held = 5 * matrix + parts * order * width + blocks * parts * rows * order
@@ -736,7 +761,7 @@
     anywhere = pl.BlockSpec(memory_space=pl.ANY)
     return pl.pallas_call(
         functools.partial(exchange_kernel, n),
-        out_shape=jax.ShapeDtypeStruct((diags, parts, rows, order), kind),
+        out_shape=jax.ShapeDtypeStruct((half, parts, rows, order), kind),
         in_specs=[smem] * 6 + [anywhere] * 6,
         out_specs=pl.BlockSpec(memory_space=pltpu.VMEM),
         scratch_shapes=[
@@ -747,17 +772,17 @@
             pltpu.VMEM((parts, order, width), kind),
             [[pltpu.VMEM((half, parts, BAND, order), kind)] * bands] * sources,
             [[pltpu.VMEM((extra, parts, BAND, order), kind)] * bands] * sources,
-            [pltpu.VMEM((max(extra, slots), sources, parts, rows, width), kind)] * chunks,
+            [[pltpu.VMEM((max(extra, slots), parts, rows, width), kind)] * chunks] * sources,
             pltpu.VMEM((chunks, half, sources, parts, rows, width), kind),
             [pltpu.VMEM((half + slots + 1, parts, rows, width), kind)] * chunks,
             [pltpu.VMEM((half + 1, sources, parts, rows, width), kind)] * chunks,
             dma,
-            dma,
+            dma((2 * bands + 1,)),
             dma((chunks,)),
             dma,
             dma((sources, bands)),
             dma((sources, bands)),
-            dma((chunks,)),
+            dma((sources, chunks)),
             dma((chunks,)),
             dma((chunks,)),
             dma((chunks,)),
@@ -776,9 +801,27 @@
             dma((chunks,)),
         ],
         compiler_params=pltpu.CompilerParams(
-            collective_id=0, has_side_effects=True, vmem_limit_bytes=held * kind.itemsize + 2**20
+            collective_id=which,
+            has_side_effects=True,
+            vmem_limit_bytes=held * kind.itemsize + 2**20,
         ),
-    )(*tables_and_rows)
+    )(*rows_in)
+
+
+def local(nodes, pair_nodes, prod_left, prod_right, prod_flag, prod_diag, *, n):
+    _, parts, rows, order = nodes.shape
+    count = prod_left.shape[0]
+    assert count == n == pair_nodes.shape[0] and rows * n == order and n % 4 == 0
+    extra, _ = plan_sizes(count)
+    small, *rows_in = plan_and_gather(
+        n, nodes, pair_nodes, prod_left, prod_right, prod_flag, prod_diag, order // WIDTH
+    )
+    whole = lambda *rows_in: exchange(n, rows_in, extra, 0)
+    if not searched(count):
+        return whole(*rows_in)
+    return lax.cond(
+        small[0] == 1, lambda *rows_in: exchange(n, rows_in, extra - 1, 1), whole, *rows_in
+    )
 
 
 def solution(mesh):

time: 328 us -> 294 us (0.90)
  Pallas kernels: 322 us -> 289 us
    pallas_call x1, Pallas kernels: 315 us -> 281 us  [exchange(): pl.pallas_call(functools.partial(exchange_kernel, n), out_shape=jax.Shape...]
where the time goes in v3:
time: 294 us; the launch traced here: 293 us
  Pallas kernels  289 us (98%)
    pallas_call x1, Pallas kernels, exchange(): pl.pallas_call(functools.partial(exchange_kernel, n), out_shape=jax.Shape...  281 us
    pallas_call x1, Pallas kernels, plan_and_gather(): pl.pallas_call(functools.partial(plan_and_gather_kernel, n), out_shape=(t...  7.62 us

profile of v3, /device:TPU:13, one launch (start us, length us, event | category | flops | bytes accessed | tf_op | source)
XLA Modules:
  0.0 292.5 jit_solution(5328193915089398629)
XLA Ops:
  0.0 0.8 slice_bitcast_fusion
  0.8 0.7 stack.19.graph
  1.5 7.6 %shard_map.66 = (s32[1]{0:T(128)}, s32[16]{0:T(128)S(1)}, s32[16]{0:T(128)S(1)}, s32[16]{0:T(128)S(1)}, s32[16]{0:T(128)S(1)}, /*index=5*/s32[24]{0:T(128)S(1)},...) custom-call(s32[6,16]{1,0:T(8,128)S(1)} %stack.19.graph, ...), custom_call_target="tpu_custom_call" | custom-call | tf_op jit(solution)/shard_map/pallas_call | solution.py:257
  9.7 281.5 %conditional.1 = (bf16[8,2,64,1024]{3,2,1,0:T(8,128)(2,1)S(1)}) conditional(s32[]{:T(128)} %bitcast.6, (s32[16]{0:T(128)S(1)}, s32[16]{0:T(128)S(1)}, s32[16]{0:T(128)S(1)}, s32[16]{0:T(128)S(1)}, s32[24]{0:T(128)S(1)}, /*index=5*/s32[32]{0:T(128)S(1)}, bf16[8,2,64,1024]{3,2,1,0:T(8,128)(2,1)S(1)}, bf16[8,2,64,1024]{3,2,1,0:T(8,128)(2,1)S(1)}, ...), branch_computations={%region_0.0_spmd, %region_1.0_spmd} | conditional | bytes 8 | solution.py:822
  10.0 280.9 %branch_1_fun.1 = bf16[8,2,64,1024]{3,2,1,0:T(8,128)(2,1)S(1)} custom-call(s32[16]{0:T(128)S(1)} %get-tuple-element.68.flags, s32[16]{0:T(128)S(1)} %get-tuple-element.69.left_slot, s32[16]{0:T(128)S(1)} %get-tuple-element.70.extra_slot, s32[16]{0:T(128)S(1)} %get-tuple-element.71.is_extra, s32[24]{0:T(128)S(1)} %get-tuple-element.72.merges, ...), custom_call_target="tpu_custom_call" | custom-call | tf_op jit(solution)/shard_map/cond/branch_1_fun/pallas_call | solution.py:762
  291.2 1.3 copy.12
